TPU v7x, 128 devices: a whole 4x4x4 slice. The times are simulated.
128 devices in a mesh: rows: 8 (over x, core), cols: 16 (over z, y).
Axes of the slice: x: 4, y: 4, z: 4, core: 2. Of those that a mesh axis runs over, the one named last changes fastest.
Arguments:
- blocks: bfloat16 [96, 96, 256, 256], P('rows', 'cols'), may hold values from -1.5 to 1.5
- pattern: int32 [96, 96], P('rows', 'cols'), may hold values 0 or 1
- pivot_inverse: bfloat16 [2, 256, 256], replicated, may hold values from -0.375 to 0.375
- right_sides: float32 [96, 3, 256], P('rows'), may hold values from -6 to 6
Outputs:
- factored: bfloat16 [96, 96, 256, 256], P('rows', 'cols')
- forward: float32 [96, 3, 256], P('rows')
All inputs are finite; a program needn't handle non-finite values. No bound on the sum of `pattern` on one device may be relied on, other than what follows from the above.
Results may differ from a plain program's by a relative error of at most 0.0071.
Values may be sent and summed in bfloat16 or wider, within the bound.
A program may use at most 128 MiB of HBM per device.

v0:
```python
import jax
import jax.numpy as jnp
from jax import lax
from jax.sharding import PartitionSpec as P


def spread(x, axis, root):
    mine = lax.axis_index(axis) == root
    return lax.psum(jnp.where(mine, x, jnp.zeros_like(x)), axis)


def schur(part, lower, upper, live_part):
    prod = jnp.einsum("iab,jbc->ijac", lower, upper, preferred_element_type=jnp.float32)
    fresh = (part.astype(jnp.float32) - prod).astype(jnp.bfloat16)
    return jnp.where(live_part[:, :, None, None], fresh, part)


def on_device(blocks, pattern, pivot_inverse, right_sides):
    row_count = blocks.shape[0]
    nrows = lax.axis_size("rows")
    ncols = lax.axis_size("cols")
    row_glob = jnp.arange(row_count) * nrows + lax.axis_index("rows")
    col_glob = jnp.arange(blocks.shape[1]) * ncols + lax.axis_index("cols")
    live = pattern == 1
    zero_block = jnp.zeros((), jnp.bfloat16)
    matrix = jnp.where(live[:, :, None, None], blocks, zero_block)

    def column_panel(column, step):
        scaled = jnp.einsum(
            "nab,bc->nac", column, pivot_inverse[step], preferred_element_type=jnp.float32
        ).astype(jnp.bfloat16)
        landed = spread(scaled, "cols", step % ncols)
        return jnp.where((row_glob > step)[:, None, None], landed, zero_block)

    def pivot_panel(rowblocks, step):
        landed = spread(rowblocks, "rows", step % nrows)
        return jnp.where((col_glob > step)[:, None, None], landed, zero_block)

    def place_lower(matrix, lower, step):
        where_lower = (col_glob == step)[None, :] & (row_glob > step)[:, None]
        return jnp.where(where_lower[:, :, None, None], lower[:, None], matrix)

    lower_zero = column_panel(matrix[:, 0], 0)
    upper_zero = pivot_panel(matrix[0], 0)
    matrix = schur(matrix, lower_zero, upper_zero, live)
    lower_one = column_panel(matrix[:, 0], 1)
    upper_one = pivot_panel(matrix[0], 1)
    matrix = place_lower(matrix, lower_zero, 0)
    matrix = schur(matrix, lower_one, upper_one, live)
    matrix = place_lower(matrix, lower_one, 1)
    first = spread(right_sides[0], "rows", 0)
    rhs = right_sides - jnp.einsum(
        "nab,cb->nca", lower_zero.astype(jnp.float32), first, precision=lax.Precision.HIGHEST
    )
    second = spread(rhs[1 // nrows], "rows", 1 % nrows)
    rhs = rhs - jnp.einsum(
        "nab,cb->nca", lower_one.astype(jnp.float32), second, precision=lax.Precision.HIGHEST
    )
    return (matrix, rhs)


def solution(mesh):
    return jax.shard_map(
        on_device,
        mesh=mesh,
        in_specs=(P("rows", "cols", None, None), P("rows", "cols"), P(), P("rows", None, None)),
        out_specs=(P("rows", "cols", None, None), P("rows", None, None)),
        check_vma=False,
    )
```

profile of v0, /device:TPU:0, one launch (start us, length us, event | category | flops | bytes accessed | tf_op | source)
XLA Modules:
  0.0 362.8 jit_solution(4188063975407825787)
XLA Ops:
  7.2 0.0 all-reduce.7.cloned.1.call-start
  7.2 0.7 broadcast_compare_fusion
  7.9 0.0 copy-start.2
  7.9 8.2 %copy_select_fusion = bf16[12,6,256,256]{3,2,0,1:T(8,128)(2,1)} fusion(bf16[12,6,256,256]{3,2,1,0:T(8,128)(2,1)} %param.4, pred[12,6]{0,1:T(8,128)(4,1)S(1)} %broadcast_compare_fusion), kind=kLoop, calls=%fused_computation.7 | loop fusion | flops 4718592 | bytes 18874440 | tf_op jit(solution)/shard_map/jit(_where)/select_n | solution.py:26
  16.1 0.0 copy-done.2
  16.1 3.1 broadcast_select_fusion.2
  19.2 0.0 all-reduce.7.cloned.1.call-update
  19.2 0.0 all-reduce.5.cloned.1.call-start
  19.3 2.1 fusion.11
  21.4 0.0 all-reduce.5.cloned.1.call-update
  21.4 0.0 all-reduce.9.cloned.1.call-start
  21.5 89.4 %all-reduce.7.cloned.1.call-done = bf16[12,256,256]{2,1,0:T(8,128)(2,1)} async-done(((bf16[12,256,256]{2,1,0:T(8,128)(2,1)}), bf16[12,256,256]{2,1,0:T(8,128)(2,1)}) %all-reduce.7.cloned.1.call-update) | async-done | bytes 1572880 | tf_op jit(solution)/shard_map/psum | solution.py:9
  110.9 1.6 broadcast_select_fusion
  112.5 62.1 %all-reduce.5.cloned.1.call-done = bf16[6,256,256]{2,1,0:T(8,128)(2,1)} async-done(((bf16[6,256,256]{2,1,0:T(8,128)(2,1)}), bf16[6,256,256]{2,1,0:T(8,128)(2,1)}) %all-reduce.5.cloned.1.call-update) | async-done | bytes 786448 | tf_op jit(solution)/shard_map/psum | solution.py:9
  174.6 6.5 %fusion.2 = bf16[12,6,256,256]{3,2,0,1:T(8,128)(2,1)S(1)} fusion(pred[12,6]{0,1:T(8,128)(4,1)S(1)} %broadcast_compare_fusion, bf16[12,256,256]{2,1,0:T(8,128)(2,1)S(1)} %broadcast_select_fusion, bf16[6,256,256]{2,1,0:T(8,128)(2,1)} %all-reduce.5.cloned.1.call-done, pred[6]{0:T(512)(128)(4,1)S(1)} %broadcast_compare_fusion.2, bf16[12,6,256,256]{3,2,1,0:T(8,128)(2,1)} %param.4), kind=kOutput, calls=%fused_computation.4 | convolution fusion | flops 2439905280 | bytes 21233742 | tf_op jit(solution)/shard_map/iab,jbc->ijac/dot_general | solution.py:13
  181.0 0.0 copy-start
  181.0 3.7 %copy-done = bf16[12,6,256,256]{3,2,0,1:T(8,128)(2,1)} copy-done((bf16[12,6,256,256]{3,2,0,1:T(8,128)(2,1)}, bf16[12,6,256,256]{3,2,0,1:T(8,128)(2,1)S(1)}, u32[]{:S(2)}) %copy-start) | copy-done | bytes 9437208
  184.8 0.0 copy-start.1
  184.8 1.7 broadcast_select_fusion.3
  186.5 0.0 all-reduce.9.cloned.1.call-update
  186.5 0.0 all-reduce.11.cloned.1.call-start
  186.6 0.0 copy-done.1
  186.6 13.4 %psum.46 = f32[3,256]{1,0:T(4,128)S(1)} all-reduce(f32[3,256]{1,0:T(4,128)S(1)} %select_bitcast_fusion), channel_id=1, replica_groups=mesh['rows'=8,'cols'=16] {'rows'}, use_global_device_ids=true, to_apply=%region_4.5 | all-reduce | flops 768 | bytes 6144 | tf_op jit(solution)/shard_map/psum | solution.py:9
  200.0 0.1 broadcast_and_fusion
  200.1 0.1 broadcast_and_fusion.1
  200.1 1.3 fusion.8
  201.4 12.7 %psum.47 = f32[3,256]{1,0:T(4,128)S(1)} all-reduce(f32[3,256]{1,0:T(4,128)S(1)} %fusion.24), channel_id=1, replica_groups=mesh['rows'=8,'cols'=16] {'rows'}, use_global_device_ids=true, to_apply=%region_5.6 | all-reduce | flops 768 | bytes 6144 | tf_op jit(solution)/shard_map/psum | solution.py:9
  214.1 2.1 fusion.9
  216.2 0.0 all-reduce.11.cloned.1.call-update
  216.2 58.7 %all-reduce.9.cloned.1.call-done = bf16[12,256,256]{2,1,0:T(8,128)(2,1)} async-done(((bf16[12,256,256]{2,1,0:T(8,128)(2,1)}), bf16[12,256,256]{2,1,0:T(8,128)(2,1)}) %all-reduce.9.cloned.1.call-update) | async-done | bytes 1572880 | tf_op jit(solution)/shard_map/psum | solution.py:9
  274.9 1.6 broadcast_select_fusion.1
  276.5 2.0 fusion.7
  278.5 59.9 %all-reduce.11.cloned.1.call-done = bf16[6,256,256]{2,1,0:T(8,128)(2,1)} async-done(((bf16[6,256,256]{2,1,0:T(8,128)(2,1)}), bf16[6,256,256]{2,1,0:T(8,128)(2,1)}) %all-reduce.11.cloned.1.call-update) | async-done | bytes 786448 | tf_op jit(solution)/shard_map/psum | solution.py:9
  338.4 9.3 %fusion.4 = bf16[12,6,256,256]{3,2,0,1:T(8,128)(2,1)} fusion(bf16[12,6,256,256]{3,2,0,1:T(8,128)(2,1)} %copy-done, pred[12,6]{0,1:T(8,128)(4,1)S(1)} %broadcast_and_fusion, pred[12,6]{0,1:T(8,128)(4,1)S(1)} %broadcast_compare_fusion, pred[12,6]{0,1:T(8,128)(4,1)S(1)} %broadcast_and_fusion.1, bf16[12,256,256]{2,1,0:T(8,128)(2,1)S(1)} %broadcast_select_fusion, ...), kind=kOutput, calls=%fused_computation.6 | convolution fusion | flops 2444623872 | bytes 22806750 | tf_op jit(solution)/shard_map/iab,jbc->ijac/dot_general | solution.py:13
  347.8 8.6 %copy.13 = bf16[12,6,256,256]{3,2,1,0:T(8,128)(2,1)} copy(bf16[12,6,256,256]{3,2,0,1:T(8,128)(2,1)} %fusion.4) | data formatting | bytes 18874368
  (7 shorter events, 0.0 us)
Async XLA Ops:
  7.2 103.7 %all-reduce.7.cloned.1.call-start = ((), (), s32[]{:S(2)}) async-start(), calls=%async_computation.1 | async-start | bytes 3145728 | tf_op jit(solution)/shard_map/psum | solution.py:9
  7.9 8.2 %copy-start.2 = (bf16[2,256,256]{2,1,0:T(8,128)(2,1)S(1)}, bf16[2,256,256]{2,1,0:T(8,128)(2,1)}, u32[]{:S(2)}) copy-start(bf16[2,256,256]{2,1,0:T(8,128)(2,1)} %param.6) | copy-start | bytes 786436
  19.2 155.3 %all-reduce.5.cloned.1.call-start = ((), (), s32[]{:S(2)}) async-start(), calls=%async_computation | async-start | bytes 1572864 | tf_op jit(solution)/shard_map/psum | solution.py:9
  21.4 253.5 %all-reduce.9.cloned.1.call-start = ((), (), s32[]{:S(2)}) async-start(), calls=%async_computation.2 | async-start | bytes 3145728 | tf_op jit(solution)/shard_map/psum | solution.py:9
  181.0 3.7 %copy-start = (bf16[12,6,256,256]{3,2,0,1:T(8,128)(2,1)}, bf16[12,6,256,256]{3,2,0,1:T(8,128)(2,1)S(1)}, u32[]{:S(2)}) copy-start(bf16[12,6,256,256]{3,2,0,1:T(8,128)(2,1)S(1)} %fusion.2) | copy-start | bytes 28311556
  184.8 1.8 copy-start.1
  186.5 151.9 %all-reduce.11.cloned.1.call-start = ((), (), s32[]{:S(2)}) async-start(), calls=%async_computation.3 | async-start | bytes 1572864 | tf_op jit(solution)/shard_map/psum | solution.py:9
Sparse Core Ops, SparseCore 0:
  19.4 91.4 all-reduce.6
  113.2 61.2 all-reduce.4
  186.6 88.2 all-reduce.8
  277.1 61.2 all-reduce.10
where the time goes:
time: 363 us
  waiting for transfers between devices  270 us (74%)
  blocking collectives  26 us (7%)
  matrix products  23.9 us (7%)
  other arithmetic  16.4 us (5%)
  between operations  13.9 us (4%)
  local copies, waits for them, and re-layouts  12.3 us (3%)
    psum x4, waiting for transfers between devices, spread(): return lax.psum(jnp.where(mine, x, jnp.zeros_like(x)), axis)  270 us
    psum x2, blocking collectives, spread(): return lax.psum(jnp.where(mine, x, jnp.zeros_like(x)), axis)  26 us
    dot_general x2, matrix products, schur(): jnp.einsum('iab,jbc->ijac', lower, upper, preferred_element_type=jnp.floa...  15.8 us
    unnamed x7, local copies, waits for them, and re-layouts  12.3 us
    select_n x1, other arithmetic, on_device(): matrix = jnp.where(live[:, :, None, None], blocks, zero_block)  8.17 us
  transfers between devices with their start and end apart: 4, of which 4 were waited for; matrix products, arithmetic and copies ran while one was open for 3% of the time, Pallas kernels for 0%

commit v1 on v0

--- a/solution.py
+++ b/solution.py
@@ -6,7 +6,8 @@
 
 def spread(x, axis, root):
     mine = lax.axis_index(axis) == root
-    return lax.psum(jnp.where(mine, x, jnp.zeros_like(x)), axis)
+    fit_task_over_axis = lambda state, comm_axis: lax.all_gather(state, comm_axis).sum(axis=0)
+    return fit_task_over_axis(jnp.where(mine, x, jnp.zeros_like(x)), axis)
 
 
 def schur(part, lower, upper, live_part):

time: 363 us -> 480 us (1.32)
  waiting for transfers between devices: 270 us -> 353 us
  other arithmetic: 16.4 us -> 48.3 us
    all_gather x0 -> x4, waiting for transfers between devices: none -> 353 us  [spread(): lax.all_gather(state, comm_axis).sum(axis=0)]
    psum x4 -> x0, waiting for transfers between devices: 270 us -> none  [spread(): return lax.psum(jnp.where(mine, x, jnp.zeros_like(x)), axis)]
    reduce_sum x0 -> x6, other arithmetic: none -> 35.9 us  [spread(): lax.all_gather(state, comm_axis).sum(axis=0)]
    all_gather x0 -> x2, blocking collectives: none -> 26.6 us  [spread(): lax.all_gather(state, comm_axis).sum(axis=0)]
    psum x2 -> x0, blocking collectives: 26 us -> none  [spread(): return lax.psum(jnp.where(mine, x, jnp.zeros_like(x)), axis)]
    unnamed x7 -> x9, local copies, waits for them, and re-layouts: 12.3 us -> 12.3 us
  transfers between devices with their start and end apart: 4 -> 4, of which waited for: 4 -> 4; matrix products, arithmetic and copies ran while one was open for 3% -> 4% of each run, Pallas kernels for 0% -> 0%
where the time goes in v1:
time: 480 us; the launch traced here: 479 us
  waiting for transfers between devices  353 us (74%)
  other arithmetic  48.3 us (10%)
  blocking collectives  26.6 us (6%)
  matrix products  25.3 us (5%)
  between operations  13.9 us (3%)
  local copies, waits for them, and re-layouts  12.3 us (3%)
    all_gather x4, waiting for transfers between devices, spread(): lax.all_gather(state, comm_axis).sum(axis=0)  353 us
    reduce_sum x6, other arithmetic, spread(): lax.all_gather(state, comm_axis).sum(axis=0)  35.9 us
    all_gather x2, blocking collectives, spread(): lax.all_gather(state, comm_axis).sum(axis=0)  26.6 us
    dot_general x2, matrix products, schur(): jnp.einsum('iab,jbc->ijac', lower, upper, preferred_element_type=jnp.floa...  15.7 us
    unnamed x9, local copies, waits for them, and re-layouts  12.3 us
  transfers between devices with their start and end apart: 4, of which 4 were waited for; matrix products, arithmetic and copies ran while one was open for 4% of the time, Pallas kernels for 0%

profile of v1, /device:TPU:0, one launch (start us, length us, event | category | flops | bytes accessed | tf_op | source)
XLA Modules:
  0.0 479.2 jit_solution(6340565999700283684)
XLA Ops:
  7.2 0.0 all-gather.7.cloned.1.call-start
  7.2 0.7 broadcast_compare_fusion
  7.9 0.0 copy-start.3
  7.9 8.2 %copy_select_fusion = bf16[12,6,256,256]{3,2,0,1:T(8,128)(2,1)} fusion(bf16[12,6,256,256]{3,2,1,0:T(8,128)(2,1)} %param.4, pred[12,6]{0,1:T(8,128)(4,1)S(1)} %broadcast_compare_fusion), kind=kLoop, calls=%fused_computation.7 | loop fusion | flops 4718592 | bytes 18874440 | tf_op jit(solution)/shard_map/jit(_where)/select_n | solution.py:27
  16.1 2.1 slice_select_fusion.1
  18.2 0.0 all-gather.7.cloned.1.call-update
  18.2 0.0 all-gather.11.cloned.1.call-start
  18.2 0.0 copy-done.3
  18.3 3.2 broadcast_select_fusion.2
  21.4 0.0 all-gather.11.cloned.1.call-update
  21.4 0.0 all-gather.9.cloned.1.call-start
  21.5 40.1 %all-gather.7.cloned.1.call-done = bf16[8,6,256,256]{3,2,0,1:T(8,128)(2,1)} async-done(((bf16[1,6,256,256]{3,2,0,1:T(8,128)(2,1)}), bf16[8,6,256,256]{3,2,0,1:T(8,128)(2,1)}) %all-gather.7.cloned.1.call-update) | async-done | bytes 6291472 | tf_op jit(solution)/shard_map/all_gather | solution.py:9
  61.6 4.8 %reduce_sum.66 = bf16[6,256,256]{2,1,0:T(8,128)(2,1)} reduce(bf16[8,6,256,256]{3,2,0,1:T(8,128)(2,1)} %all-gather.7.cloned.1.call-done, bf16[]{:T(256)} %constant.15.clone.1), dimensions={0}, to_apply=%region_0.1 | reduce | flops 2752512 | bytes 7077890 | tf_op jit(solution)/shard_map/reduce_sum | solution.py:9
  66.5 151.7 %all-gather.11.cloned.1.call-done = bf16[192,256,256]{2,1,0:T(8,128)(2,1)} async-done(((bf16[12,256,256]{2,1,0:T(8,128)(2,1)}), bf16[192,256,256]{2,1,0:T(8,128)(2,1)}) %all-gather.11.cloned.1.call-update) | async-done | bytes 25165840 | tf_op jit(solution)/shard_map/all_gather | solution.py:9
  218.1 13.1 %reduce_sum.67 = bf16[12,256,256]{2,1,0:T(8,128)(2,1)S(1)} reduce(bf16[16,12,256,256]{3,2,1,0:T(8,128)(2,1)} %bitcast.67, bf16[]{:T(256)} %constant.15.clone.1), dimensions={0}, to_apply=%region_1.2 | reduce | flops 11796480 | bytes 26738690 | tf_op jit(solution)/shard_map/reduce_sum | solution.py:9
  231.2 0.2 broadcast_select_fusion
  231.4 6.5 %fusion.2 = bf16[12,6,256,256]{3,2,0,1:T(8,128)(2,1)S(1)} fusion(pred[12,6]{0,1:T(8,128)(4,1)S(1)} %broadcast_compare_fusion, bf16[12,256,256]{2,1,0:T(8,128)(2,1)S(1)} %broadcast_select_fusion, bf16[6,256,256]{2,1,0:T(8,128)(2,1)} %reduce_sum.66, pred[6]{0:T(512)(128)(4,1)S(1)} %broadcast_compare_fusion.2, bf16[12,6,256,256]{3,2,1,0:T(8,128)(2,1)} %param.4), kind=kOutput, calls=%fused_computation.4 | convolution fusion | flops 2439905280 | bytes 21233742 | tf_op jit(solution)/shard_map/iab,jbc->ijac/dot_general | solution.py:14
  237.9 0.0 copy-start.1
  237.9 3.7 copy-done.1
  241.6 0.0 copy-start.2
  241.6 1.0 slice_select_fusion
  242.6 0.0 all-gather.9.cloned.1.call-update
  242.6 0.0 all-gather.13.cloned.1.call-start
  242.7 3.2 broadcast_select_fusion.3
  245.8 0.0 all-gather.13.cloned.1.call-update
  245.9 0.0 copy-done.2
  245.9 13.3 %all_gather.34 = f32[8,3,256]{2,1,0:T(4,128)S(1)} all-gather(f32[1,3,256]{2,1,0:T(4,128)S(1)} %slice_select_fusion.3), channel_id=1, replica_groups=mesh['rows'=8,'cols'=16] {'rows'}, dimensions={0}, use_global_device_ids=true | all-gather | bytes 27648 | tf_op jit(solution)/shard_map/all_gather | solution.py:9
  259.3 0.1 broadcast_and_fusion
  259.3 0.1 broadcast_and_fusion.1
  259.4 1.3 fusion.8
  260.7 13.3 %all_gather.35 = f32[8,3,256]{2,1,0:T(4,128)S(1)} all-gather(f32[1,3,256]{2,1,0:T(4,128)S(1)} %slice_select_fusion.2), channel_id=1, replica_groups=mesh['rows'=8,'cols'=16] {'rows'}, dimensions={0}, use_global_device_ids=true | all-gather | bytes 27648 | tf_op jit(solution)/shard_map/all_gather | solution.py:9
  274.0 9.3 %all-gather.9.cloned.1.call-done = bf16[8,6,256,256]{3,2,0,1:T(8,128)(2,1)} async-done(((bf16[1,6,256,256]{3,2,0,1:T(8,128)(2,1)}), bf16[8,6,256,256]{3,2,0,1:T(8,128)(2,1)}) %all-gather.9.cloned.1.call-update) | async-done | bytes 6291472 | tf_op jit(solution)/shard_map/all_gather | solution.py:9
  283.3 4.8 %reduce_sum.69 = bf16[6,256,256]{2,1,0:T(8,128)(2,1)} reduce(bf16[8,6,256,256]{3,2,0,1:T(8,128)(2,1)} %all-gather.9.cloned.1.call-done, bf16[]{:T(256)} %constant.15.clone.1), dimensions={0}, to_apply=%region_3.4 | reduce | flops 2752512 | bytes 7077890 | tf_op jit(solution)/shard_map/reduce_sum | solution.py:9
  288.2 151.5 %all-gather.13.cloned.1.call-done = bf16[192,256,256]{2,1,0:T(8,128)(2,1)} async-done(((bf16[12,256,256]{2,1,0:T(8,128)(2,1)}), bf16[192,256,256]{2,1,0:T(8,128)(2,1)}) %all-gather.13.cloned.1.call-update) | async-done | bytes 25165840 | tf_op jit(solution)/shard_map/all_gather | solution.py:9
  439.6 13.1 %reduce_sum.68 = bf16[12,256,256]{2,1,0:T(8,128)(2,1)S(1)} reduce(bf16[16,12,256,256]{3,2,1,0:T(8,128)(2,1)} %bitcast.66, bf16[]{:T(256)} %constant.15.clone.1), dimensions={0}, to_apply=%region_2.3 | reduce | flops 11796480 | bytes 26738690 | tf_op jit(solution)/shard_map/reduce_sum | solution.py:9
  452.7 0.0 copy-start
  452.7 0.2 broadcast_select_fusion.1
  452.9 2.0 fusion.7
  454.9 0.0 copy-done
  454.9 9.3 %fusion.4 = bf16[12,6,256,256]{3,2,0,1:T(8,128)(2,1)} fusion(bf16[12,6,256,256]{3,2,0,1:T(8,128)(2,1)} %copy-done.1, pred[12,6]{0,1:T(8,128)(4,1)S(1)} %broadcast_and_fusion, pred[12,6]{0,1:T(8,128)(4,1)S(1)} %broadcast_compare_fusion, pred[12,6]{0,1:T(8,128)(4,1)S(1)} %broadcast_and_fusion.1, bf16[12,256,256]{2,1,0:T(8,128)(2,1)S(1)} %broadcast_select_fusion, ...), kind=kOutput, calls=%fused_computation.6 | convolution fusion | flops 2444623872 | bytes 22806750 | tf_op jit(solution)/shard_map/iab,jbc->ijac/dot_general | solution.py:14
  464.1 8.6 %copy.15 = bf16[12,6,256,256]{3,2,1,0:T(8,128)(2,1)} copy(bf16[12,6,256,256]{3,2,0,1:T(8,128)(2,1)} %fusion.4) | data formatting | bytes 18874368
  (9 shorter events, 0.1 us)
Async XLA Ops:
  7.2 54.5 %all-gather.7.cloned.1.call-start = ((), (), s32[]{:S(2)}) async-start(), calls=%async_computation | async-start | bytes 7077888 | tf_op jit(solution)/shard_map/all_gather | solution.py:9
  7.9 10.3 %copy-start.3 = (bf16[2,256,256]{2,1,0:T(8,128)(2,1)S(1)}, bf16[2,256,256]{2,1,0:T(8,128)(2,1)}, u32[]{:S(2)}) copy-start(bf16[2,256,256]{2,1,0:T(8,128)(2,1)} %param.6) | copy-start | bytes 786436
  18.2 199.9 %all-gather.11.cloned.1.call-start = ((), (), s32[]{:S(2)}) async-start(), calls=%async_computation.2 | async-start | bytes 26738688 | tf_op jit(solution)/shard_map/all_gather | solution.py:9
  21.4 261.9 %all-gather.9.cloned.1.call-start = ((), (), s32[]{:S(2)}) async-start(), calls=%async_computation.1 | async-start | bytes 7077888 | tf_op jit(solution)/shard_map/all_gather | solution.py:9
  237.9 3.7 copy-start.1
  241.6 4.2 copy-start.2
  242.6 197.0 %all-gather.13.cloned.1.call-start = ((), (), s32[]{:S(2)}) async-start(), calls=%async_computation.3 | async-start | bytes 26738688 | tf_op jit(solution)/shard_map/all_gather | solution.py:9
  452.7 2.1 copy-start
Sparse Core Ops, SparseCore 0:
  18.3 43.2 all-gather.6
  63.8 154.3 all-gather.10
  242.7 40.5 all-gather.8
  285.3 154.2 all-gather.12
